TPU v7x, 32 devices: a whole 2x2x4 slice. The times are simulated.
32 devices in a mesh: expert: 8 (over z, x), hidden: 4 (over y, core).
Axes of the slice: x: 2, y: 2, z: 4, core: 2. Of those that a mesh axis runs over, the one named last changes fastest.
Arguments:
- tokens: bfloat16 [16384, 768], P(('expert', 'hidden')), may hold values from -6 to 6
- doc_lengths: int32 [8, 3], P('expert'), may hold values from 1 to 1024, 2048 in all within a row
- expert_ids: int32 [16384, 2], P(('expert', 'hidden')), may hold values from 0 to 7, all different within a row; in each aligned block of 512 rows (0 to 511, 512 to 1023, ...) at most 160 rows name the same one
- gain_one: float32 [768], replicated, may hold values from 0.5 to 1.5
- shift_one: float32 [768], replicated, may hold values from -1.25 to 1.25
- w_query: bfloat16 [768, 768], replicated, may hold values from -0.21875 to 0.21875
- w_key: bfloat16 [768, 768], replicated, may hold values from -0.21875 to 0.21875
- w_value: bfloat16 [768, 768], replicated, may hold values from -0.21875 to 0.21875
- w_out: bfloat16 [768, 768], replicated, may hold values from -3.5 to 3.5
- gain_two: float32 [768], replicated, may hold values from 0.5 to 1.5
- shift_two: float32 [768], replicated, may hold values from -1.25 to 1.25
- w_router: bfloat16 [768, 8], replicated, may hold values from -0.21875 to 0.21875
- w_up: bfloat16 [8, 768, 3072], P('expert', None, 'hidden'), may hold values from -0.21875 to 0.21875
- w_down: bfloat16 [8, 3072, 768], P('expert', 'hidden'), may hold values from -0.109375 to 0.109375
- out_grad: bfloat16 [16384, 768], P(('expert', 'hidden')), may hold values from -6 to 6
Outputs:
- output: bfloat16 [16384, 768], P(('expert', 'hidden'))
- input_grad: bfloat16 [16384, 768], P(('expert', 'hidden'))
- gain_one_grad: float32 [768], replicated
- shift_one_grad: float32 [768], replicated
- w_query_grad: float32 [768, 768], replicated
- w_key_grad: float32 [768, 768], replicated
- w_value_grad: float32 [768, 768], replicated
- w_out_grad: float32 [768, 768], replicated
- gain_two_grad: float32 [768], replicated
- shift_two_grad: float32 [768], replicated
- w_router_grad: float32 [768, 8], replicated
- w_up_grad: float32 [8, 768, 3072], P('expert', None, 'hidden')
- w_down_grad: float32 [8, 3072, 768], P('expert', 'hidden')
- load: float32 [8], replicated
Inputs may be any that keep to these rules, and one draw needn't show every extreme that they name: `doc_lengths`: the lengths of a group's documents, in order; they sum to 2048 and the longest in every group is 1024. `expert_ids`: each token names 2 different experts; among the 512 tokens of one device no expert is named more than 160 times, and in every draw some expert is named exactly 160 times by one device.
All inputs are finite; a program needn't handle non-finite values.
Results may differ from a plain program's by a relative error of at most 0.019.
Values may be sent and summed in bfloat16 or wider, within the bound.
A program may use at most 192 MiB of HBM per device.

v0:
```python
from functools import partial
import jax
import jax.numpy as jnp
from jax import lax
from jax.sharding import PartitionSpec as P

HEADS = 12
HEAD_DIM = 64
EPSILON = 1e-05
SCALE = 0.125
MASKED = -1e30
EXACT = lax.Precision.HIGHEST


def product(left, right):
    return jnp.dot(left, right, preferred_element_type=jnp.float32)


def contract(left, right, left_axis, right_axis):
    return lax.dot_general(
        left, right, (((left_axis,), (right_axis,)), ((), ())), preferred_element_type=jnp.float32
    )


def norm_parts(values):
    row_mean = jnp.mean(values, axis=-1, keepdims=True)
    centred = values - row_mean
    inverse = lax.rsqrt(jnp.mean(centred * centred, axis=-1, keepdims=True) + EPSILON)
    return (centred * inverse, inverse)


def norm_back(grad_out, normed, inverse, gain):
    grad_normed = grad_out * gain
    first_mean = jnp.mean(grad_normed, axis=-1, keepdims=True)
    second_mean = jnp.mean(grad_normed * normed, axis=-1, keepdims=True)
    return inverse * (grad_normed - first_mean - normed * second_mean)


def gelu_back(pre_act, grad_hidden):
    unused, pull = jax.vjp(partial(jax.nn.gelu, approximate=True), pre_act)
    return pull(grad_hidden)[0]


def split_heads(array):
    return array.reshape(array.shape[0], HEADS, HEAD_DIM).transpose(1, 0, 2)


def join_heads(array):
    return array.transpose(1, 0, 2).reshape(array.shape[1], HEADS * HEAD_DIM)


def shards(
    tokens,
    doc_lengths,
    expert_ids,
    gain_one,
    shift_one,
    w_query,
    w_key,
    w_value,
    w_out,
    gain_two,
    shift_two,
    w_router,
    w_up,
    w_down,
    out_grad,
):
    row_count = tokens.shape[0]
    model_width = tokens.shape[1]
    top_count = expert_ids.shape[1]
    experts = lax.axis_size("expert") * w_up.shape[0]
    capacity = max(2, row_count * top_count * 5 // (4 * experts))
    input_float = tokens.astype(jnp.float32)
    normed_one, inverse_one = norm_parts(input_float)
    h_one = (normed_one * gain_one + shift_one).astype(jnp.bfloat16)
    queries = product(h_one, w_query).astype(jnp.bfloat16)
    key_proj = product(h_one, w_key).astype(jnp.bfloat16)
    value_proj = product(h_one, w_value).astype(jnp.bfloat16)
    all_keys, all_values = (
        lax.all_gather(key_proj, "hidden", axis=0, tiled=True),
        lax.all_gather(value_proj, "hidden", axis=0, tiled=True),
    )
    key_count = all_keys.shape[0]
    doc_ends = jnp.cumsum(doc_lengths[0])
    query_pos = lax.axis_index("hidden") * row_count + jnp.arange(row_count, dtype=jnp.int32)
    key_pos = jnp.arange(key_count, dtype=jnp.int32)
    query_doc = jnp.sum((query_pos[:, None] >= doc_ends[None, :]).astype(jnp.int32), axis=1)
    key_doc = jnp.sum((key_pos[:, None] >= doc_ends[None, :]).astype(jnp.int32), axis=1)
    allowed = (query_doc[:, None] == key_doc[None, :]) & (key_pos[None, :] <= query_pos[:, None])

    def head_forward(pieces):
        q_head, k_head, v_head = pieces
        scores = jnp.where(allowed, contract(q_head, k_head, 1, 1) * SCALE, MASKED)
        top_score = jnp.max(scores, axis=1, keepdims=True)
        expd = jnp.exp(scores - top_score)
        row_total = jnp.sum(expd, axis=1, keepdims=True)
        weights = (expd / row_total).astype(jnp.bfloat16)
        return (product(weights, v_head), (top_score + jnp.log(row_total))[:, 0])

    mixture, log_total = lax.map(
        head_forward, (split_heads(queries), split_heads(all_keys), split_heads(all_values))
    )
    attended = join_heads(mixture).astype(jnp.bfloat16)
    residual = input_float + product(attended, w_out)
    normed_two, inverse_two = norm_parts(residual)
    h_two = (normed_two * gain_two + shift_two).astype(jnp.bfloat16)
    h_two_float = h_two.astype(jnp.float32)
    router_float = w_router.astype(jnp.float32)
    logits = jnp.dot(h_two_float, router_float, precision=EXACT)
    choose_table = (
        expert_ids[:, :, None] == jnp.arange(experts, dtype=jnp.int32)[None, None, :]
    ).astype(jnp.float32)
    chosen = jnp.sum(choose_table * logits[:, None, :], axis=2)
    gate_weights = jax.nn.softmax(chosen, axis=1)
    flat_ids = expert_ids.reshape(-1)
    onehot = choose_table.reshape(-1, experts).astype(jnp.int32)
    before = jnp.cumsum(onehot, axis=0) - onehot
    slot_index = jnp.sum(before * onehot, axis=1)
    counts = jnp.sum(choose_table, axis=(0, 1))
    outgoing = (
        jnp.zeros((experts, capacity, model_width), jnp.bfloat16)
        .at[flat_ids, slot_index]
        .set(jnp.repeat(h_two, top_count, axis=0))
    )
    slot_rows = lax.all_to_all(outgoing, "expert", split_axis=0, concat_axis=0, tiled=True).reshape(
        -1, model_width
    )
    rows_all = lax.all_gather(slot_rows, "hidden", axis=0, tiled=True)
    pre_act = product(rows_all, w_up[0])
    hidden_act = jax.nn.gelu(pre_act, approximate=True).astype(jnp.bfloat16)
    partial_sum = product(hidden_act, w_down[0])
    produced = lax.psum_scatter(
        partial_sum.astype(jnp.bfloat16), "hidden", scatter_dimension=0, tiled=True
    )
    returned = lax.all_to_all(
        produced.reshape(-1, capacity, model_width),
        "expert",
        split_axis=0,
        concat_axis=0,
        tiled=True,
    )
    returned_rows = (
        returned[flat_ids, slot_index]
        .reshape(row_count, top_count, model_width)
        .astype(jnp.float32)
    )
    expert_mix = jnp.sum(gate_weights[:, :, None] * returned_rows, axis=1)
    output = (residual + expert_mix).astype(jnp.bfloat16)
    grad_output = out_grad.astype(jnp.float32)
    grad_returned = (gate_weights[:, :, None] * grad_output[:, None, :]).astype(jnp.bfloat16)
    grad_gates = jnp.sum(returned_rows * grad_output[:, None, :], axis=2)
    grad_chosen = gate_weights * (
        grad_gates - jnp.sum(gate_weights * grad_gates, axis=1, keepdims=True)
    )
    grad_logits = jnp.sum(grad_chosen[:, :, None] * choose_table, axis=1)
    router_grad = jnp.dot(h_two_float.T, grad_logits, precision=EXACT)
    grad_h_two = jnp.dot(grad_logits, router_float.T, precision=EXACT)
    grad_outgoing = (
        jnp.zeros((experts, capacity, model_width), jnp.bfloat16)
        .at[flat_ids, slot_index]
        .set(grad_returned.reshape(-1, model_width))
    )
    grad_slots = lax.all_to_all(
        grad_outgoing, "expert", split_axis=0, concat_axis=0, tiled=True
    ).reshape(-1, model_width)
    trainable = (lax.axis_index("expert") >= experts // 2).astype(jnp.float32)
    grad_all = lax.all_gather(grad_slots, "hidden", axis=0, tiled=True)
    grad_hidden = contract(grad_all, w_down[0], 1, 1)
    down_grad = contract(hidden_act, grad_all, 0, 0)
    grad_pre = gelu_back(pre_act, grad_hidden).astype(jnp.bfloat16)
    up_grad = contract(rows_all, grad_pre, 0, 0)
    partial_in = contract(grad_pre, w_up[0], 1, 1)
    grad_in = lax.psum_scatter(
        partial_in.astype(jnp.bfloat16), "hidden", scatter_dimension=0, tiled=True
    )
    up_grad = up_grad[None] * trainable
    down_grad = down_grad[None] * trainable
    grad_back = lax.all_to_all(
        grad_in.reshape(-1, capacity, model_width),
        "expert",
        split_axis=0,
        concat_axis=0,
        tiled=True,
    )
    grad_h_two = grad_h_two + jnp.sum(
        grad_back[flat_ids, slot_index]
        .reshape(row_count, top_count, model_width)
        .astype(jnp.float32),
        axis=1,
    )
    gain_two_grad = jnp.sum(grad_h_two * normed_two, axis=0)
    shift_two_grad = jnp.sum(grad_h_two, axis=0)
    grad_residual = grad_output + norm_back(grad_h_two, normed_two, inverse_two, gain_two)
    grad_branch = grad_residual.astype(jnp.bfloat16)
    out_proj_grad = contract(attended, grad_branch, 0, 0)
    grad_attended = contract(grad_branch, w_out, 1, 1).astype(jnp.bfloat16)
    back_keys, back_values = (all_keys, all_values)

    def head_backward(pieces):
        q_head, k_head, v_head, g_head, head_total = pieces
        scores = jnp.where(allowed, contract(q_head, k_head, 1, 1) * SCALE, MASKED)
        weights = jnp.exp(scores - head_total[:, None])
        grad_weights = contract(g_head, v_head, 1, 1)
        grad_scores = (
            weights * (grad_weights - jnp.sum(weights * grad_weights, axis=1, keepdims=True))
        ).astype(jnp.bfloat16)
        grad_query = product(grad_scores, k_head) * SCALE
        grad_key = contract(grad_scores, q_head, 0, 0) * SCALE
        grad_value = contract(weights.astype(jnp.bfloat16), g_head, 0, 0)
        return (grad_query, grad_key, grad_value)

    grad_query, grad_key, grad_value = lax.map(
        head_backward,
        (
            split_heads(queries),
            split_heads(back_keys),
            split_heads(back_values),
            split_heads(grad_attended),
            log_total,
        ),
    )
    grad_key, grad_value = (
        lax.psum_scatter(
            join_heads(grad_key).astype(jnp.bfloat16), "hidden", scatter_dimension=0, tiled=True
        ).astype(jnp.float32),
        lax.psum_scatter(
            join_heads(grad_value).astype(jnp.bfloat16), "hidden", scatter_dimension=0, tiled=True
        ).astype(jnp.float32),
    )
    grad_query = join_heads(grad_query).astype(jnp.bfloat16)
    grad_key = grad_key.astype(jnp.bfloat16)
    grad_value = grad_value.astype(jnp.bfloat16)
    query_grad = contract(h_one, grad_query, 0, 0)
    key_grad = contract(h_one, grad_key, 0, 0)
    value_grad = contract(h_one, grad_value, 0, 0)
    grad_h_one = (
        contract(grad_query, w_query, 1, 1)
        + contract(grad_key, w_key, 1, 1)
        + contract(grad_value, w_value, 1, 1)
    )
    gain_one_grad = jnp.sum(grad_h_one * normed_one, axis=0)
    shift_one_grad = jnp.sum(grad_h_one, axis=0)
    input_grad = (grad_residual + norm_back(grad_h_one, normed_one, inverse_one, gain_one)).astype(
        jnp.bfloat16
    )
    totals = lax.psum(
        (
            gain_one_grad,
            shift_one_grad,
            query_grad,
            key_grad,
            value_grad,
            out_proj_grad,
            gain_two_grad,
            shift_two_grad,
            router_grad,
            counts,
        ),
        ("expert", "hidden"),
    )
    total_tokens = row_count * lax.axis_size("expert") * lax.axis_size("hidden")
    load = totals[9] * experts / (total_tokens * top_count)
    return (
        output,
        input_grad,
        totals[0],
        totals[1],
        totals[2],
        totals[3],
        totals[4],
        totals[5],
        totals[6],
        totals[7],
        totals[8],
        up_grad,
        down_grad,
        load,
    )


def solution(mesh):
    in_specs = (
        P(("expert", "hidden"), None),
        P("expert", None),
        P(("expert", "hidden"), None),
        P(),
        P(),
        P(),
        P(),
        P(),
        P(),
        P(),
        P(),
        P(),
        P("expert", None, "hidden"),
        P("expert", "hidden", None),
        P(("expert", "hidden"), None),
    )
    out_specs = (
        P(("expert", "hidden"), None),
        P(("expert", "hidden"), None),
        P(),
        P(),
        P(),
        P(),
        P(),
        P(),
        P(),
        P(),
        P(),
        P("expert", None, "hidden"),
        P("expert", "hidden", None),
        P(),
    )
    return jax.shard_map(shards, mesh=mesh, in_specs=in_specs, out_specs=out_specs, check_vma=False)
```

profile of v0, /device:TPU:0, one launch (start us, length us, event | category | flops | bytes accessed | tf_op | source)
XLA Modules:
  0.0 1053.0 jit_solution(8360045255467511472)
XLA Ops:
  10.2 3.5 convolution_convert_fusion.4
  32.1 13.0 %all-gather.5.cloned.1.call-done = bf16[2048,768]{1,0:T(8,128)(2,1)} async-done(((bf16[512,768]{1,0:T(8,128)(2,1)}), bf16[2048,768]{1,0:T(8,128)(2,1)}) %all-gather.5.cloned.1.call-update) | async-done | bytes 3145744 | tf_op jit(solution)/shard_map/all_gather | solution.py:81
  45.1 4.8 copy.68
  49.9 6.7 copy.71
  56.6 19.4 %all-gather.7.cloned.1.call-done = bf16[2048,768]{1,0:T(8,128)(2,1)} async-done(((bf16[512,768]{1,0:T(8,128)(2,1)}), bf16[2048,768]{1,0:T(8,128)(2,1)}) %all-gather.7.cloned.1.call-update) | async-done | bytes 3145744 | tf_op jit(solution)/shard_map/all_gather | solution.py:82
  76.0 4.7 copy.69
  80.7 6.5 copy.72
  88.2 85.5 %while.28 = (s32[]{:T(128)}, bf16[12,512,64]{1,2,0:T(8,128)(2,1)}, f32[12,512]{1,0:T(8,128)}, bf16[12,512,64]{2,1,0:T(8,128)(2,1)S(1)}, bf16[12,2048,64]{2,1,0:T...) while((s32[]{:T(128)}, bf16[12,512,64]{1,2,0:T(8,128)(2,1)}, ...), condition=%wide.region_8.9_spmd.clone, body=%wide.region_5.8_spmd.clone.sunk | while | flops 279969280 | bytes 13928569 | solution.py:101
  98.3 2.7 fusion.149
  105.4 2.7 fusion.149
  112.6 2.7 fusion.149
  119.7 2.7 fusion.149
  126.8 2.7 fusion.149
  133.9 2.7 fusion.149
  141.1 2.7 fusion.149
  155.3 2.7 fusion.149
  169.5 2.7 fusion.149
  173.6 3.0 fusion.95
  181.0 7.7 scatter_custom_fusion
  188.8 51.8 %all_to_all.20 = bf16[8,160,768]{2,1,0:T(8,128)(2,1)} all-to-all(bf16[8,160,768]{2,1,0:T(8,128)(2,1)} %bitcast.191), channel_id=1, replica_groups=mesh['expert'=8,'hidden'=4] {'expert'}, dimensions={0} | all-to-all | bytes 3932160 | tf_op jit(solution)/shard_map/all_to_all | solution.py:126
  244.2 5.5 mul.265
  250.5 7.0 scatter_custom_fusion.1
  257.5 48.8 %all_to_all.21 = bf16[8,160,768]{2,1,0:T(8,128)(2,1)} all-to-all(bf16[8,160,768]{2,1,0:T(8,128)(2,1)S(1)} %bitcast.190), channel_id=1, replica_groups=mesh['expert'=8,'hidden'=4] {'expert'}, dimensions={0} | all-to-all | bytes 3932160 | tf_op jit(solution)/shard_map/all_to_all | solution.py:164
  306.6 12.8 %fusion.72 = f32[5120,768]{1,0:T(8,128)} fusion(bf16[5120,768]{1,0:T(8,128)(2,1)} %all-gather.9.cloned.1.call-done, bf16[1,768,768]{2,1,0:T(8,128)(2,1)S(1)} %copy-done), kind=kOutput, calls=%fused_computation.115 | convolution fusion | flops 6039797760 | bytes 24772608 | tf_op jit(solution)/shard_map/dot_general | solution.py:16
  319.4 40.1 %all-gather.11.cloned.1.call-done = bf16[5120,768]{1,0:T(8,128)(2,1)} async-done(((bf16[1280,768]{1,0:T(8,128)(2,1)}), bf16[5120,768]{1,0:T(8,128)(2,1)}) %all-gather.11.cloned.1.call-update) | async-done | bytes 7864336 | tf_op jit(solution)/shard_map/all_gather | solution.py:168
  359.5 19.0 %fusion.50 = bf16[5120,768]{1,0:T(8,128)(2,1)S(1)} fusion(f32[5120,768]{1,0:T(8,128)} %fusion.72, bf16[5120,768]{1,0:T(8,128)(2,1)} %all-gather.11.cloned.1.call-done, bf16[1,768,768]{2,1,0:T(8,128)(2,1)S(1)} %copy-done.40), kind=kOutput, calls=%fused_computation.67 | convolution fusion | flops 6118440960 | bytes 32636928 | tf_op jit(solution)/shard_map/dot_general | solution.py:20
  378.5 3.1 copy-done.48
  381.7 8.7 convolution_convert_fusion
  390.5 14.8 %convolution_convert_fusion.1 = bf16[5120,768]{1,0:T(8,128)(2,1)} fusion(bf16[1,768,768]{2,1,0:T(8,128)(2,1)S(1)} %copy-done.40, f32[5120,768]{1,0:T(8,128)} %fusion.72), kind=kOutput, calls=%fused_computation.70 | convolution fusion | flops 6079119360 | bytes 24772608 | tf_op jit(solution)/shard_map/dot_general | solution.py:16
  405.3 54.2 %reduce-scatter.7.cloned.1.call-done = bf16[1280,768]{1,0:T(8,128)(2,1)} async-done(((bf16[5120,768]{1,0:T(8,128)(2,1)}), bf16[1280,768]{1,0:T(8,128)(2,1)}) %reduce-scatter.7.cloned.1.call-update) | async-done | bytes 1966096 | tf_op jit(solution)/shard_map/reduce_scatter | solution.py:174
  459.5 5.5 all-to-all-start.3
  465.0 66.1 %reduce-scatter.5.cloned.1.call-done = bf16[1280,768]{1,0:T(8,128)(2,1)} async-done(((bf16[5120,768]{1,0:T(8,128)(2,1)}), bf16[1280,768]{1,0:T(8,128)(2,1)}) %reduce-scatter.5.cloned.1.call-update) | async-done | bytes 1966096 | tf_op jit(solution)/shard_map/reduce_scatter | solution.py:133
  531.1 5.6 all-to-all-start.1
  538.1 14.3 %gather_fusion.1 = bf16[1024,768]{1,0:T(8,128)(2,1)} fusion(bf16[8,160,768]{2,1,0:T(8,128)(2,1)S(1)} %all-to-all-done.3, s32[1024]{0:T(1024)S(1)} %bitcast.184), kind=kCustom, calls=%fused_computation.1 | custom fusion | bytes 3153920 | tf_op jit(solution)/shard_map/gather | solution.py:187
  552.4 4.9 reshape.365
  557.3 25.0 %all-to-all-done.1 = bf16[8,160,768]{2,1,0:T(8,128)(2,1)} async-done(((bf16[8,160,768]{2,1,0:T(8,128)(2,1)}), bf16[8,160,768]{2,1,0:T(8,128)(2,1)}, u32[]{:S(2)}, u32[]{:S(2)}) %all-to-all-start.1) | async-done | bytes 1966112 | tf_op jit(solution)/shard_map/all_to_all | solution.py:136
  582.3 19.8 %gather_fusion = bf16[1024,768]{1,0:T(8,128)(2,1)} fusion(bf16[8,160,768]{2,1,0:T(8,128)(2,1)} %all-to-all-done.1, s32[1024]{0:T(1024)S(1)} %bitcast.185), kind=kCustom, calls=%fused_computation | custom fusion | bytes 3153920 | tf_op jit(solution)/shard_map/gather | solution.py:144
  602.1 3.5 reshape.364
  605.6 9.5 multiply_reduce_fusion.1
  616.4 5.7 reduce_sum.241
  626.7 132.8 %while.29 = (s32[]{:T(128)}, bf16[12,512,64]{1,2,0:T(8,128)(2,1)S(1)}, bf16[12,2048,64]{1,2,0:T(8,128)(2,1)}, bf16[12,2048,64]{1,2,0:T(8,128)(2,1)}, bf16[12,512...) while((s32[]{:T(128)}, ...), condition=%wide.region_30.31_spmd.clone, body=%wide.region_28.30_spmd.clone.sunk | while | flops 683834880 | bytes 34630792 | solution.py:213
  629.3 2.9 multiply_reduce_fusion.11
  640.3 2.9 multiply_reduce_fusion.11
  651.4 3.0 multiply_reduce_fusion.11
  662.4 3.0 multiply_reduce_fusion.11
  673.5 3.0 multiply_reduce_fusion.11
  684.6 3.0 multiply_reduce_fusion.11
  695.7 2.9 multiply_reduce_fusion.11
  706.7 3.0 multiply_reduce_fusion.11
  717.8 2.9 multiply_reduce_fusion.11
  728.9 2.9 multiply_reduce_fusion.11
  739.9 2.9 multiply_reduce_fusion.11
  751.0 3.0 multiply_reduce_fusion.11
  761.0 3.7 fusion.89
  766.8 28.9 %reduce-scatter.9.cloned.1.call-done = bf16[512,768]{0,1:T(8,128)(2,1)} async-done(((bf16[2048,768]{0,1:T(8,128)(2,1)}), bf16[512,768]{0,1:T(8,128)(2,1)}) %reduce-scatter.9.cloned.1.call-update) | async-done | bytes 786448 | tf_op jit(solution)/shard_map/reduce_scatter | solution.py:224
  795.7 3.6 fusion.87
  799.3 37.1 %reduce-scatter.11.cloned.1.call-done = bf16[512,768]{0,1:T(8,128)(2,1)} async-done(((bf16[2048,768]{0,1:T(8,128)(2,1)}), bf16[512,768]{0,1:T(8,128)(2,1)}) %reduce-scatter.11.cloned.1.call-update) | async-done | bytes 786448 | tf_op jit(solution)/shard_map/reduce_scatter | solution.py:227
  836.4 3.6 fusion.85
  840.0 12.2 %multiply_bitcast_fusion.1 = f32[1,768,768]{2,1,0:T(8,128)} fusion(bf16[5120,768]{1,0:T(8,128)(2,1)} %all-gather.9.cloned.1.call-done, bf16[5120,768]{1,0:T(8,128)(2,1)} %copy-done.48, f32[]{:T(128)S(6)} %convert_element_type.180), kind=kOutput, calls=%fused_computation.78 | convolution fusion | flops 6040387584 | bytes 18087940 | tf_op jit(solution)/shard_map/dot_general | solution.py:20
  852.2 14.4 %multiply_bitcast_fusion = f32[1,768,768]{2,1,0:T(8,128)} fusion(bf16[5120,768]{1,0:T(8,128)(2,1)} %all-gather.11.cloned.1.call-done, f32[]{:T(128)S(6)} %convert_element_type.180, f32[5120,768]{1,0:T(8,128)} %fusion.72), kind=kOutput, calls=%fused_computation.77 | convolution fusion | flops 6075777024 | bytes 25952260 | tf_op jit(solution)/shard_map/dot_general | solution.py:20
  872.6 41.3 %all-reduce = (f32[768]{0:T(1024)}, f32[768]{0:T(1024)}, f32[768]{0:T(1024)}, f32[768]{0:T(1024)}, f32[768,8]{0,1:T(8,128)}, /*index=5*/f32[8]{0:T(128)S(1)}) all-reduce(f32[768]{0:T(1024)S(1)} %get-tuple-element.230, f32[768]{0:T(1024)S(1)} %get-tuple-element.235, ...), channel_id=1, replica_groups=mesh['expert'=8,'hidden'=4] {'expert','hidden'}, use_global_device_ids=true, to_apply=%region_36.37 | all-reduce | flops 9224 | bytes 73792 | tf_op jit(solution)/shard_map/psum | solution.py:247
  914.4 2.9 fusion.63
  917.3 119.2 %all-reduce.4.cloned.1.call-done = (f32[768,768]{1,0:T(8,128)}, f32[768,768]{1,0:T(8,128)}, f32[768,768]{1,0:T(8,128)}, f32[768,768]{1,0:T(8,128)}) async-done(((f32[768,768]{1,0:T(8,128)}, f32[768,768]{1,0:T(8,128)}, f32[768,768]{1,0:T(8,128)}, f32[768,768]{1,0:T(8,128)}), (f32[768,768]{1,0:T(8,128)}, f32[768,768]{1,0:T(8,128)}, f32[768,768]{1,0:T(8,128)}, ...) | async-done | bytes 9437200 | tf_op jit(solution)/shard_map/psum | solution.py:247
  1036.5 3.4 copy.121
  (306 shorter events, 212.7 us)
Async XLA Ops:
  7.2 299.4 %copy-start = (bf16[1,768,768]{2,1,0:T(8,128)(2,1)S(1)}, bf16[1,768,768]{2,1,0:T(8,128)(2,1)}, u32[]{:S(2)}) copy-start(bf16[1,768,768]{2,1,0:T(8,128)(2,1)} %param.31) | copy-start | bytes 3538948
  7.2 37.9 %all-gather.5.cloned.1.call-start = ((), (), s32[]{:S(2)}) async-start(), calls=%async_computation.8 | async-start | bytes 3932160 | tf_op jit(solution)/shard_map/all_gather | solution.py:81
  8.6 12.4 %copy-start.26 = (f32[512]{0:T(512)}, f32[512]{0:T(512)S(1)}, u32[]{:S(2)}) copy-start(f32[512]{0:T(512)S(1)} %broadcast_multiply_fusion.5) | copy-start | bytes 6148
  10.2 10.9 %copy-start.30 = (f32[512]{0:T(512)}, f32[512]{0:T(512)S(1)}, u32[]{:S(2)}) copy-start(f32[512]{0:T(512)S(1)} %add_rsqrt_fusion.1) | copy-start | bytes 6148
  10.2 3.6 copy-start.4
  10.2 3.6 copy-start.17
  10.2 3.6 copy-start.32
  10.2 3.6 copy-start.45
  13.7 2.3 copy-start.25
  13.7 3.6 copy-start.47
  13.7 62.2 %all-gather.7.cloned.1.call-start = ((), (), s32[]{:S(2)}) async-start(), calls=%async_computation.9 | async-start | bytes 3932160 | tf_op jit(solution)/shard_map/all_gather | solution.py:82
  15.7 290.9 %all-gather.9.cloned.1.call-start = ((), (), s32[]{:S(2)}) async-start(), calls=%async_computation.10 | async-start | bytes 9830400 | tf_op jit(solution)/shard_map/all_gather | solution.py:129
  20.3 0.6 copy-start.22
  23.2 3.2 copy-start.39
  26.4 5.1 copy-start.34
  80.7 7.5 copy-start.35
  173.6 3.0 copy-start.12
  173.6 4.7 copy-start.24
  173.6 4.7 copy-start.38
  176.7 1.1 copy-start.2
  177.8 0.6 copy-start.28
  178.7 71.0 %copy-start.6 = (bf16[512,768]{1,0:T(8,128)(2,1)}, bf16[512,768]{1,0:T(8,128)(2,1)S(1)}, u32[]{:S(2)}) copy-start(bf16[512,768]{1,0:T(8,128)(2,1)S(1)} %add_convert_fusion.1) | copy-start | bytes 2359300
  240.6 1.1 copy-start.8
  240.6 118.9 %all-gather.11.cloned.1.call-start = ((), (), s32[]{:S(2)}) async-start(), calls=%async_computation.12 | async-start | bytes 9830400 | tf_op jit(solution)/shard_map/all_gather | solution.py:168
  244.2 5.5 copy-start.23
  306.3 53.2 %copy-start.40 = (bf16[1,768,768]{2,1,0:T(8,128)(2,1)S(1)}, bf16[1,768,768]{2,1,0:T(8,128)(2,1)}, u32[]{:S(2)}) copy-start(bf16[1,768,768]{2,1,0:T(8,128)(2,1)} %param.32) | copy-start | bytes 3538948
  306.3 153.2 %reduce-scatter.7.cloned.1.call-start = ((), (), s32[]{:S(2)}) async-start(), calls=%async_computation.13 | async-start | bytes 9830400 | tf_op jit(solution)/shard_map/reduce_scatter | solution.py:174
  378.5 3.2 copy-start.48
  390.4 140.7 %reduce-scatter.5.cloned.1.call-start = ((), (), s32[]{:S(2)}) async-start(), calls=%async_computation.11 | async-start | bytes 9830400 | tf_op jit(solution)/shard_map/reduce_scatter | solution.py:133
  459.5 71.6 %all-to-all-start.3 = ((bf16[8,160,768]{2,1,0:T(8,128)(2,1)}), bf16[8,160,768]{2,1,0:T(8,128)(2,1)S(1)}, u32[]{:S(2)}, u32[]{:S(2)}) async-start(bf16[8,160,768]{2,1,0:T(8,128)(2,1)} %bitcast.199), calls=%async_computation.5 | async-start | bytes 3932160 | tf_op jit(solution)/shard_map/all_to_all | solution.py:179
  531.1 5.7 copy-start.9
  531.1 51.2 %all-to-all-start.1 = ((bf16[8,160,768]{2,1,0:T(8,128)(2,1)}), bf16[8,160,768]{2,1,0:T(8,128)(2,1)}, u32[]{:S(2)}, u32[]{:S(2)}) async-start(bf16[8,160,768]{2,1,0:T(8,128)(2,1)} %bitcast.198), calls=%async_computation.2 | async-start | bytes 3932160 | tf_op jit(solution)/shard_map/all_to_all | solution.py:136
  536.8 258.9 %reduce-scatter.9.cloned.1.call-start = ((), (), s32[]{:S(2)}) async-start(), calls=%async_computation.14 | async-start | bytes 3932160 | tf_op jit(solution)/shard_map/reduce_scatter | solution.py:224
  616.3 5.7 copy-start.3
  616.3 5.8 copy-start.29
  622.1 1.4 copy-start.10
  622.1 1.6 copy-start.11
  623.8 1.4 copy-start.41
  626.0 0.7 copy-start.36
  626.0 0.7 copy-start.37
  759.5 0.9 copy-start.20
  759.5 1.4 copy-start.5
  759.5 1.4 copy-start.27
  759.5 1.4 copy-start.31
  759.6 1.4 copy-start.33
  759.6 1.4 copy-start.46
  759.6 76.8 %reduce-scatter.11.cloned.1.call-start = ((), (), s32[]{:S(2)}) async-start(), calls=%async_computation.15 | async-start | bytes 3932160 | tf_op jit(solution)/shard_map/reduce_scatter | solution.py:227
  760.4 276.1 %all-reduce.4.cloned.1.call-start = ((), (), s32[]{:S(2)}) async-start(), calls=%async_computation.16 | async-start | bytes 18874368 | tf_op jit(solution)/shard_map/psum | solution.py:247
  760.9 3.7 copy-start.13
  852.2 14.4 %copy-start.7 = (bf16[512,768]{1,0:T(8,128)(2,1)S(1)}, bf16[512,768]{1,0:T(8,128)(2,1)}, u32[]{:S(2)}) copy-start(bf16[512,768]{1,0:T(8,128)(2,1)} %copy-done.6) | copy-start | bytes 2359300
  852.2 14.8 %copy-start.21 = (bf16[12,512,64]{1,2,0:T(8,128)(2,1)S(1)}, bf16[12,512,64]{1,2,0:T(8,128)(2,1)}, u32[]{:S(2)}) copy-start(bf16[12,512,64]{1,2,0:T(8,128)(2,1)} %copy-done.20) | copy-start | bytes 2359300
  852.2 14.8 %copy-start.42 = (bf16[768,768]{1,0:T(8,128)(2,1)S(1)}, bf16[768,768]{1,0:T(8,128)(2,1)}, u32[]{:S(2)}) copy-start(bf16[768,768]{1,0:T(8,128)(2,1)} %param.24) | copy-start | bytes 3538948
  867.0 1.3 copy-start.43
  867.0 1.5 copy-start.44
  868.5 1.3 copy-start.18
  868.5 1.5 copy-start.19
  1036.5 3.4 copy-start.16
  1039.8 2.5 copy-start.15
  1042.4 2.5 copy-start.14
  1042.4 3.9 copy-start.1
Sparse Core Ops, SparseCore 0:
  13.8 31.2 all-gather.4
  47.2 28.6 all-gather.6
  240.7 53.0 all-gather.8
  306.4 53.0 all-gather.10
  390.5 68.9 reduce-scatter.6
  462.1 68.9 reduce-scatter.4
  759.6 36.0 reduce-scatter.8
  798.4 37.9 reduce-scatter.10
  843.2 193.2 all-reduce.3
where the time goes:
time: 1060 us; the launch traced here: 1050 us
  waiting for transfers between devices  404 us (38%)
  matrix products  292 us (28%)
  blocking collectives  142 us (13%)
  local copies, waits for them, and re-layouts  134 us (13%)
  other arithmetic  54.7 us (5%)
  between operations  14.7 us (1%)
  starting transfers between devices  11.9 us (1%)
    dot_general x72, matrix products, contract(): lax.dot_general(left, right, (((left_axis,), (right_axis,)), ((), ())), p...  197 us
    psum x1, waiting for transfers between devices, shards(): lax.psum((gain_one_grad, shift_one_grad, query_grad, key_grad, value_grad...  119 us
    dot_general x30, matrix products, product(): return jnp.dot(left, right, preferred_element_type=jnp.float32)  92.8 us
    reduce_scatter x1, waiting for transfers between devices, shards(): lax.psum_scatter(partial_sum.astype(jnp.bfloat16), 'hidden', scatter_dime...  66.1 us
    reduce_scatter x1, waiting for transfers between devices, shards(): lax.psum_scatter(partial_in.astype(jnp.bfloat16), 'hidden', scatter_dimen...  54.2 us
    all_to_all x1, blocking collectives, shards(): lax.all_to_all(outgoing, 'expert', split_axis=0, concat_axis=0, tiled=True)  51.8 us
    all_to_all x1, blocking collectives, shards(): lax.all_to_all(grad_outgoing, 'expert', split_axis=0, concat_axis=0, tile...  48.8 us
    unnamed x107, local copies, waits for them, and re-layouts  41.6 us
  transfers between devices with their start and end apart: 11, of which 9 were waited for; matrix products, arithmetic and copies ran while one was open for 13% of the time, Pallas kernels for 0%

commit v1 on v0

--- a/solution.py
+++ b/solution.py
@@ -3,6 +3,7 @@
 import jax.numpy as jnp
 from jax import lax
 from jax.sharding import PartitionSpec as P
+from jax.lax import axis_index, axis_size, ppermute
 
 HEADS = 12
 HEAD_DIM = 64
@@ -165,7 +166,26 @@
         grad_outgoing, "expert", split_axis=0, concat_axis=0, tiled=True
     ).reshape(-1, model_width)
     trainable = (lax.axis_index("expert") >= experts // 2).astype(jnp.float32)
-    grad_all = lax.all_gather(grad_slots, "hidden", axis=0, tiled=True)
+    a_now, arr_out, x_now = (axis_size("hidden"), axis_index("hidden"), grad_slots.shape[0])
+    pool = tuple((q * a_now if num == 0 else q for num, q in enumerate(grad_slots.shape)))
+    grad_all = lax.dynamic_update_slice_in_dim(
+        jnp.zeros(pool, grad_slots.dtype), grad_slots, arr_out * x_now, axis=0
+    )
+    oldest = u1 = grad_slots
+    ix = 1
+    while ix < a_now // 2 + 1:
+        oldest = ppermute(
+            oldest, "hidden", tuple(((num, (num + 1) % a_now) for num in range(a_now)))
+        )
+        grad_all = lax.dynamic_update_slice_in_dim(
+            grad_all, oldest, (arr_out - ix) % a_now * x_now, axis=0
+        )
+        if 2 * ix < a_now:
+            u1 = ppermute(u1, "hidden", tuple(((num, (num - 1) % a_now) for num in range(a_now))))
+            grad_all = lax.dynamic_update_slice_in_dim(
+                grad_all, u1, (arr_out + ix) % a_now * x_now, axis=0
+            )
+        ix += 1
     grad_hidden = contract(grad_all, w_down[0], 1, 1)
     down_grad = contract(hidden_act, grad_all, 0, 0)
     grad_pre = gelu_back(pre_act, grad_hidden).astype(jnp.bfloat16)

time: 1060 us -> 1090 us (1.028)
  local copies, waits for them, and re-layouts: 134 us -> 147 us
  waiting for transfers between devices: 404 us -> 415 us
    ppermute x0 -> x3, waiting for transfers between devices: none -> 54.6 us  [the longest x2 54.6 us: shards(): ppermute(oldest, 'hidden', tuple(((num, (num + 1) % a_now) for num in ran...]
    all_gather x1 -> x0, waiting for transfers between devices: 40.1 us -> none  [shards(): grad_all = lax.all_gather(grad_slots, 'hidden', axis=0, tiled=True)]
    dynamic_update_slice x0 -> x4, local copies, waits for them, and re-layouts: none -> 11.9 us  [the longest x2 5.93 us: shards(): lax.dynamic_update_slice_in_dim(grad_all, oldest, (arr_out - ix) % a_now...]
    unnamed x107 -> x123, local copies, waits for them, and re-layouts: 41.6 us -> 41.4 us
  transfers between devices with their start and end apart: 11 -> 13, of which waited for: 9 -> 10; matrix products, arithmetic and copies ran while one was open for 13% -> 13% of each run, Pallas kernels for 0% -> 0%
where the time goes in v1:
time: 1090 us; the launch traced here: 1080 us
  waiting for transfers between devices  415 us (38%)
  matrix products  293 us (27%)
  local copies, waits for them, and re-layouts  147 us (13%)
  blocking collectives  142 us (13%)
  other arithmetic  57.3 us (5%)
  between operations  15 us (1%)
  starting transfers between devices  13.4 us (1%)
    dot_general x72, matrix products, contract(): lax.dot_general(left, right, (((left_axis,), (right_axis,)), ((), ())), p...  196 us
    psum x1, waiting for transfers between devices, shards(): lax.psum((gain_one_grad, shift_one_grad, query_grad, key_grad, value_grad...  119 us
    dot_general x30, matrix products, product(): return jnp.dot(left, right, preferred_element_type=jnp.float32)  93.4 us
    reduce_scatter x1, waiting for transfers between devices, shards(): lax.psum_scatter(partial_sum.astype(jnp.bfloat16), 'hidden', scatter_dime...  66.1 us
    ppermute x2, waiting for transfers between devices, shards(): ppermute(oldest, 'hidden', tuple(((num, (num + 1) % a_now) for num in ran...  54.6 us
    all_to_all x1, blocking collectives, shards(): lax.all_to_all(outgoing, 'expert', split_axis=0, concat_axis=0, tiled=True)  51.8 us
    reduce_scatter x1, waiting for transfers between devices, shards(): lax.psum_scatter(partial_in.astype(jnp.bfloat16), 'hidden', scatter_dimen...  49.5 us
    all_to_all x1, blocking collectives, shards(): lax.all_to_all(grad_outgoing, 'expert', split_axis=0, concat_axis=0, tile...  49.3 us
  transfers between devices with their start and end apart: 13, of which 10 were waited for; matrix products, arithmetic and copies ran while one was open for 13% of the time, Pallas kernels for 0%

profile of v1, /device:TPU:0, one launch (start us, length us, event | category | flops | bytes accessed | tf_op | source)
XLA Modules:
  0.0 1082.8 jit_solution(18068115985048139838)
XLA Ops:
  10.2 3.5 convolution_convert_fusion.4
  31.3 13.8 %all-gather.4.cloned.1.call-done = bf16[2048,768]{1,0:T(8,128)(2,1)} async-done(((bf16[512,768]{1,0:T(8,128)(2,1)}), bf16[2048,768]{1,0:T(8,128)(2,1)}) %all-gather.4.cloned.1.call-update) | async-done | bytes 3145744 | tf_op jit(solution)/shard_map/all_gather | solution.py:82
  45.1 4.8 copy.68
  49.9 6.7 copy.71
  56.6 19.2 %all-gather.6.cloned.1.call-done = bf16[2048,768]{1,0:T(8,128)(2,1)} async-done(((bf16[512,768]{1,0:T(8,128)(2,1)}), bf16[2048,768]{1,0:T(8,128)(2,1)}) %all-gather.6.cloned.1.call-update) | async-done | bytes 3145744 | tf_op jit(solution)/shard_map/all_gather | solution.py:83
  75.8 4.7 copy.69
  80.5 6.5 copy.72
  88.0 85.2 %while.28 = (s32[]{:T(128)}, bf16[12,512,64]{1,2,0:T(8,128)(2,1)}, f32[12,512]{1,0:T(8,128)}, bf16[12,512,64]{2,1,0:T(8,128)(2,1)S(1)}, bf16[12,2048,64]{2,1,0:T...) while((s32[]{:T(128)}, bf16[12,512,64]{1,2,0:T(8,128)(2,1)}, ...), condition=%wide.region_8.9_spmd.clone, body=%wide.region_5.8_spmd.clone.sunk | while | flops 279969280 | bytes 13928569 | solution.py:102
  91.0 2.7 fusion.149
  98.1 2.7 fusion.149
  140.7 2.7 fusion.149
  179.5 4.6 reshape.380
  184.1 7.8 scatter_custom_fusion
  191.9 51.8 %all_to_all.20 = bf16[8,160,768]{2,1,0:T(8,128)(2,1)} all-to-all(bf16[8,160,768]{2,1,0:T(8,128)(2,1)} %bitcast.190), channel_id=1, replica_groups=mesh['expert'=8,'hidden'=4] {'expert'}, dimensions={0} | all-to-all | bytes 3932160 | tf_op jit(solution)/shard_map/all_to_all | solution.py:127
  243.7 3.6 mul.270
  247.3 5.5 mul.277
  254.9 7.8 scatter_custom_fusion.1
  262.7 49.3 %all_to_all.21 = bf16[8,160,768]{2,1,0:T(8,128)(2,1)} all-to-all(bf16[8,160,768]{2,1,0:T(8,128)(2,1)} %bitcast.189), channel_id=1, replica_groups=mesh['expert'=8,'hidden'=4] {'expert'}, dimensions={0} | all-to-all | bytes 3932160 | tf_op jit(solution)/shard_map/all_to_all | solution.py:165
  313.8 42.8 %collective-permute-done = bf16[1280,768]{1,0:T(8,128)(2,1)} collective-permute-done((bf16[1280,768]{1,0:T(8,128)(2,1)}, bf16[1280,768]{1,0:T(8,128)(2,1)}, u32[]{:S(2)}, u32[]{:S(2)}) %collective-permute-start) | collective-permute-done | bytes 1966112 | tf_op jit(solution)/shard_map/ppermute | solution.py:177
  356.6 3.7 broadcast_in_dim.32
  360.3 2.9 constant_dynamic-update-slice_fusion.3
  363.2 3.0 constant_dynamic-update-slice_fusion.2
  366.2 3.0 constant_dynamic-update-slice_fusion.1
  369.2 11.8 %collective-permute-done.2 = bf16[1280,768]{1,0:T(8,128)(2,1)} collective-permute-done((bf16[1280,768]{1,0:T(8,128)(2,1)}, bf16[1280,768]{1,0:T(8,128)(2,1)}, u32[]{:S(2)}, u32[]{:S(2)}) %collective-permute-start.2) | collective-permute-done | bytes 1966112 | tf_op jit(solution)/shard_map/ppermute | solution.py:177
  381.0 2.9 constant_dynamic-update-slice_fusion
  384.0 12.8 %fusion.72 = f32[5120,768]{1,0:T(8,128)} fusion(bf16[5120,768]{1,0:T(8,128)(2,1)} %all-gather.8.cloned.1.call-done, bf16[1,768,768]{2,1,0:T(8,128)(2,1)S(1)} %copy-done), kind=kOutput, calls=%fused_computation.115 | convolution fusion | flops 6039797760 | bytes 24772608 | tf_op jit(solution)/shard_map/dot_general | solution.py:17
  396.7 19.0 %fusion.50 = bf16[5120,768]{1,0:T(8,128)(2,1)S(1)} fusion(f32[5120,768]{1,0:T(8,128)} %fusion.72, bf16[5120,768]{1,0:T(8,128)(2,1)} %constant_dynamic-update-slice_fusion, bf16[1,768,768]{2,1,0:T(8,128)(2,1)S(1)} %copy-done.47), kind=kOutput, calls=%fused_computation.67 | convolution fusion | flops 6118440960 | bytes 32636928 | tf_op jit(solution)/shard_map/dot_general | solution.py:21
  415.7 3.2 copy-done.56
  418.9 8.6 convolution_convert_fusion
  428.8 16.1 %convolution_convert_fusion.1 = bf16[5120,768]{1,0:T(8,128)(2,1)} fusion(bf16[1,768,768]{2,1,0:T(8,128)(2,1)S(1)} %copy-done.48, f32[5120,768]{1,0:T(8,128)} %fusion.72), kind=kOutput, calls=%fused_computation.70 | convolution fusion | flops 6079119360 | bytes 24772608 | tf_op jit(solution)/shard_map/dot_general | solution.py:17
  444.9 49.5 %reduce-scatter.7.cloned.1.call-done = bf16[1280,768]{1,0:T(8,128)(2,1)} async-done(((bf16[5120,768]{1,0:T(8,128)(2,1)}), bf16[1280,768]{1,0:T(8,128)(2,1)}) %reduce-scatter.7.cloned.1.call-update) | async-done | bytes 1966096 | tf_op jit(solution)/shard_map/reduce_scatter | solution.py:194
  494.4 5.5 all-to-all-start.3
  500.0 66.1 %reduce-scatter.5.cloned.1.call-done = bf16[1280,768]{1,0:T(8,128)(2,1)} async-done(((bf16[5120,768]{1,0:T(8,128)(2,1)}), bf16[1280,768]{1,0:T(8,128)(2,1)}) %reduce-scatter.5.cloned.1.call-update) | async-done | bytes 1966096 | tf_op jit(solution)/shard_map/reduce_scatter | solution.py:134
  566.0 5.5 all-to-all-start.1
  574.0 14.3 %gather_fusion.1 = bf16[1024,768]{1,0:T(8,128)(2,1)} fusion(bf16[8,160,768]{2,1,0:T(8,128)(2,1)S(1)} %all-to-all-done.3, s32[1024]{0:T(1024)S(1)} %bitcast.184), kind=kCustom, calls=%fused_computation.1 | custom fusion | bytes 3153920 | tf_op jit(solution)/shard_map/gather | solution.py:207
  588.3 4.9 reshape.365
  593.2 23.9 %all-to-all-done.1 = bf16[8,160,768]{2,1,0:T(8,128)(2,1)} async-done(((bf16[8,160,768]{2,1,0:T(8,128)(2,1)}), bf16[8,160,768]{2,1,0:T(8,128)(2,1)}, u32[]{:S(2)}, u32[]{:S(2)}) %all-to-all-start.1) | async-done | bytes 1966112 | tf_op jit(solution)/shard_map/all_to_all | solution.py:137
  617.1 14.6 %gather_fusion = bf16[1024,768]{1,0:T(8,128)(2,1)S(1)} fusion(bf16[8,160,768]{2,1,0:T(8,128)(2,1)} %all-to-all-done.1, s32[1024]{0:T(1024)S(1)} %bitcast.185), kind=kCustom, calls=%fused_computation | custom fusion | bytes 3153920 | tf_op jit(solution)/shard_map/gather | solution.py:145
  631.7 2.7 reshape.364
  634.4 9.7 multiply_reduce_fusion.1
  645.0 5.6 reduce_sum.241
  655.6 133.3 %while.29 = (s32[]{:T(128)}, bf16[12,512,64]{1,2,0:T(8,128)(2,1)S(1)}, bf16[12,2048,64]{1,2,0:T(8,128)(2,1)}, bf16[12,2048,64]{1,2,0:T(8,128)(2,1)}, bf16[12,512...) while((s32[]{:T(128)}, ...), condition=%wide.region_30.31_spmd.clone, body=%wide.region_28.30_spmd.clone.sunk | while | flops 683834880 | bytes 34630792 | solution.py:233
  658.1 3.0 multiply_reduce_fusion.11
  669.3 3.0 multiply_reduce_fusion.11
  680.4 3.0 multiply_reduce_fusion.11
  691.5 3.0 multiply_reduce_fusion.11
  702.6 3.0 multiply_reduce_fusion.11
  713.7 3.0 multiply_reduce_fusion.11
  724.9 3.0 multiply_reduce_fusion.11
  736.0 3.0 multiply_reduce_fusion.11
  747.1 3.0 multiply_reduce_fusion.11
  758.2 3.0 multiply_reduce_fusion.11
  769.3 3.0 multiply_reduce_fusion.11
  780.4 3.0 multiply_reduce_fusion.11
  794.9 30.4 %reduce-scatter.9.cloned.1.call-done = bf16[512,768]{0,1:T(8,128)(2,1)} async-done(((bf16[2048,768]{0,1:T(8,128)(2,1)}), bf16[512,768]{0,1:T(8,128)(2,1)}) %reduce-scatter.9.cloned.1.call-update) | async-done | bytes 786448 | tf_op jit(solution)/shard_map/reduce_scatter | solution.py:244
  825.2 3.6 fusion.87
  828.8 37.1 %reduce-scatter.11.cloned.1.call-done = bf16[512,768]{0,1:T(8,128)(2,1)} async-done(((bf16[2048,768]{0,1:T(8,128)(2,1)}), bf16[512,768]{0,1:T(8,128)(2,1)}) %reduce-scatter.11.cloned.1.call-update) | async-done | bytes 786448 | tf_op jit(solution)/shard_map/reduce_scatter | solution.py:247
  865.9 3.6 fusion.85
  869.6 12.2 %multiply_bitcast_fusion.1 = f32[1,768,768]{2,1,0:T(8,128)} fusion(bf16[5120,768]{1,0:T(8,128)(2,1)} %all-gather.8.cloned.1.call-done, bf16[5120,768]{1,0:T(8,128)(2,1)} %copy-done.56, f32[]{:T(128)S(6)} %convert_element_type.180), kind=kOutput, calls=%fused_computation.78 | convolution fusion | flops 6040387584 | bytes 18087940 | tf_op jit(solution)/shard_map/dot_general | solution.py:21
  881.8 14.4 %multiply_bitcast_fusion = f32[1,768,768]{2,1,0:T(8,128)} fusion(bf16[5120,768]{1,0:T(8,128)(2,1)} %constant_dynamic-update-slice_fusion, f32[]{:T(128)S(6)} %convert_element_type.180, f32[5120,768]{1,0:T(8,128)} %fusion.72), kind=kOutput, calls=%fused_computation.77 | convolution fusion | flops 6075777024 | bytes 25952260 | tf_op jit(solution)/shard_map/dot_general | solution.py:21
  902.2 41.3 %all-reduce = (f32[768]{0:T(1024)}, f32[768]{0:T(1024)}, f32[768]{0:T(1024)}, f32[768]{0:T(1024)}, f32[768,8]{0,1:T(8,128)}, /*index=5*/f32[8]{0:T(128)S(1)}) all-reduce(f32[768]{0:T(1024)S(1)} %get-tuple-element.230, f32[768]{0:T(1024)S(1)} %get-tuple-element.235, ...), channel_id=1, replica_groups=mesh['expert'=8,'hidden'=4] {'expert','hidden'}, use_global_device_ids=true, to_apply=%region_36.37 | all-reduce | flops 9224 | bytes 73792 | tf_op jit(solution)/shard_map/psum | solution.py:267
  944.0 2.9 fusion.63
  946.9 119.1 %all-reduce.4.cloned.1.call-done = (f32[768,768]{1,0:T(8,128)}, f32[768,768]{1,0:T(8,128)}, f32[768,768]{1,0:T(8,128)}, f32[768,768]{1,0:T(8,128)}) async-done(((f32[768,768]{1,0:T(8,128)}, f32[768,768]{1,0:T(8,128)}, f32[768,768]{1,0:T(8,128)}, f32[768,768]{1,0:T(8,128)}), (f32[768,768]{1,0:T(8,128)}, f32[768,768]{1,0:T(8,128)}, f32[768,768]{1,0:T(8,128)}, ...) | async-done | bytes 9437200 | tf_op jit(solution)/shard_map/psum | solution.py:267
  1066.0 3.4 copy.125
  (330 shorter events, 233.7 us)
Async XLA Ops:
  7.2 376.8 %copy-start = (bf16[1,768,768]{2,1,0:T(8,128)(2,1)S(1)}, bf16[1,768,768]{2,1,0:T(8,128)(2,1)}, u32[]{:S(2)}) copy-start(bf16[1,768,768]{2,1,0:T(8,128)(2,1)} %param.31) | copy-start | bytes 3538948
  7.2 37.9 %all-gather.4.cloned.1.call-start = ((), (), s32[]{:S(2)}) async-start(), calls=%async_computation.8 | async-start | bytes 3932160 | tf_op jit(solution)/shard_map/all_gather | solution.py:82
  8.6 11.8 %copy-start.27 = (f32[512]{0:T(512)}, f32[512]{0:T(512)S(1)}, u32[]{:S(2)}) copy-start(f32[512]{0:T(512)S(1)} %broadcast_multiply_fusion.5) | copy-start | bytes 6148
  10.2 10.3 copy-start.33
  10.2 3.6 copy-start.3
  10.2 3.6 copy-start.16
  10.2 3.6 copy-start.37
  10.2 3.6 copy-start.53
  13.7 2.3 copy-start.25
  13.7 3.0 copy-start.55
  13.7 62.1 %all-gather.6.cloned.1.call-start = ((), (), s32[]{:S(2)}) async-start(), calls=%async_computation.9 | async-start | bytes 3932160 | tf_op jit(solution)/shard_map/all_gather | solution.py:83
  15.6 368.3 %all-gather.8.cloned.1.call-start = ((), (), s32[]{:S(2)}) async-start(), calls=%async_computation.10 | async-start | bytes 9830400 | tf_op jit(solution)/shard_map/all_gather | solution.py:130
  25.6 5.1 copy-start.39
  80.5 7.5 copy-start.40
  173.2 1.1 copy-start.9
  173.2 3.6 copy-start.44
  174.4 2.8 copy-start.23
  174.4 2.8 copy-start.43
  177.2 2.3 copy-start.31
  177.5 75.3 %copy-start.5 = (bf16[512,768]{1,0:T(8,128)(2,1)}, bf16[512,768]{1,0:T(8,128)(2,1)S(1)}, u32[]{:S(2)}) copy-start(bf16[512,768]{1,0:T(8,128)(2,1)S(1)} %add_convert_fusion.1) | copy-start | bytes 2359300
  243.7 250.8 %reduce-scatter.7.cloned.1.call-start = ((), (), s32[]{:S(2)}) async-start(), calls=%async_computation.12 | async-start | bytes 9830400 | tf_op jit(solution)/shard_map/reduce_scatter | solution.py:194
  254.7 8.0 copy-start.14
  312.1 44.6 %collective-permute-start = (bf16[1280,768]{1,0:T(8,128)(2,1)}, bf16[1280,768]{1,0:T(8,128)(2,1)}, u32[]{:S(2)}, u32[]{:S(2)}) collective-permute-start(bf16[1280,768]{1,0:T(8,128)(2,1)} %bitcast.19), channel_id=1, source_target_pairs={{0,1},{1,2},{2,3},{3,0},{4,5},{5,6},{6,7},{7,4},{8,9},{9,10},{10,1... | collective-permute-start | bytes 5898248 | tf_op jit(solution)/shard_map/ppermute | solution.py:177
  312.1 54.2 %collective-permute-start.1 = (bf16[1280,768]{1,0:T(8,128)(2,1)}, bf16[1280,768]{1,0:T(8,128)(2,1)}, u32[]{:S(2)}, u32[]{:S(2)}) collective-permute-start(bf16[1280,768]{1,0:T(8,128)(2,1)} %bitcast.19), channel_id=1, source_target_pairs={{0,3},{1,0},{2,1},{3,2},{4,7},{5,4},{6,5},{7,6},{8,11},{9,8},{10,9... | collective-permute-start | bytes 5898248 | tf_op jit(solution)/shard_map/ppermute | solution.py:184
  356.6 24.4 %collective-permute-start.2 = (bf16[1280,768]{1,0:T(8,128)(2,1)}, bf16[1280,768]{1,0:T(8,128)(2,1)}, u32[]{:S(2)}, u32[]{:S(2)}) collective-permute-start(bf16[1280,768]{1,0:T(8,128)(2,1)} %collective-permute-done), channel_id=1, source_target_pairs={{0,1},{1,2},{2,3},{3,0},{4,5},{5,6},{6,7},{7,4},{8,9},{9,10},{10,1... | collective-permute-start | bytes 5898248 | tf_op jit(solution)/shard_map/ppermute | solution.py:177
  384.0 12.8 %copy-start.47 = (bf16[1,768,768]{2,1,0:T(8,128)(2,1)S(1)}, bf16[1,768,768]{2,1,0:T(8,128)(2,1)}, u32[]{:S(2)}) copy-start(bf16[1,768,768]{2,1,0:T(8,128)(2,1)} %param.32) | copy-start | bytes 3538948
  415.7 3.2 copy-start.56
  427.5 1.3 copy-start.48
  427.6 138.5 %reduce-scatter.5.cloned.1.call-start = ((), (), s32[]{:S(2)}) async-start(), calls=%async_computation.11 | async-start | bytes 9830400 | tf_op jit(solution)/shard_map/reduce_scatter | solution.py:134
  494.4 71.6 %all-to-all-start.3 = ((bf16[8,160,768]{2,1,0:T(8,128)(2,1)}), bf16[8,160,768]{2,1,0:T(8,128)(2,1)S(1)}, u32[]{:S(2)}, u32[]{:S(2)}) async-start(bf16[8,160,768]{2,1,0:T(8,128)(2,1)} %bitcast.198), calls=%async_computation.5 | async-start | bytes 3932160 | tf_op jit(solution)/shard_map/all_to_all | solution.py:199
  566.0 51.0 %all-to-all-start.1 = ((bf16[8,160,768]{2,1,0:T(8,128)(2,1)}), bf16[8,160,768]{2,1,0:T(8,128)(2,1)}, u32[]{:S(2)}, u32[]{:S(2)}) async-start(bf16[8,160,768]{2,1,0:T(8,128)(2,1)} %bitcast.197), calls=%async_computation.2 | async-start | bytes 3932160 | tf_op jit(solution)/shard_map/all_to_all | solution.py:137
  571.5 2.4 copy-start.2
  571.5 253.7 %reduce-scatter.9.cloned.1.call-start = ((), (), s32[]{:S(2)}) async-start(), calls=%async_computation.13 | async-start | bytes 3932160 | tf_op jit(solution)/shard_map/reduce_scatter | solution.py:244
  631.7 2.8 copy-start.15
  634.4 9.8 copy-start.30
  634.4 9.9 copy-start.26
  645.0 5.6 copy-start.20
  645.0 5.6 copy-start.22
  645.0 5.7 copy-start.24
  645.0 5.7 copy-start.32
  650.7 1.9 copy-start.7
  650.7 1.9 copy-start.8
  652.6 1.5 copy-start.49
  789.0 1.1 copy-start.4
  789.0 1.1 copy-start.28
  789.0 1.1 copy-start.34
  789.0 1.1 copy-start.38
  789.1 76.9 %reduce-scatter.11.cloned.1.call-start = ((), (), s32[]{:S(2)}) async-start(), calls=%async_computation.14 | async-start | bytes 3932160 | tf_op jit(solution)/shard_map/reduce_scatter | solution.py:247
  789.8 276.1 %all-reduce.4.cloned.1.call-start = ((), (), s32[]{:S(2)}) async-start(), calls=%async_computation.15 | async-start | bytes 18874368 | tf_op jit(solution)/shard_map/psum | solution.py:267
  790.2 2.5 copy-start.10
  881.8 14.4 %copy-start.6 = (bf16[512,768]{1,0:T(8,128)(2,1)S(1)}, bf16[512,768]{1,0:T(8,128)(2,1)}, u32[]{:S(2)}) copy-start(bf16[512,768]{1,0:T(8,128)(2,1)} %copy-done.5) | copy-start | bytes 2359300
  881.8 14.4 %copy-start.21 = (f32[512,8]{0,1:T(8,128)S(1)}, f32[512,8]{0,1:T(8,128)}, u32[]{:S(2)}) copy-start(f32[512,8]{0,1:T(8,128)} %copy-done.20) | copy-start | bytes 49156
  881.8 14.8 %copy-start.50 = (bf16[768,768]{1,0:T(8,128)(2,1)S(1)}, bf16[768,768]{1,0:T(8,128)(2,1)}, u32[]{:S(2)}) copy-start(bf16[768,768]{1,0:T(8,128)(2,1)} %param.24) | copy-start | bytes 3538948
  896.5 1.3 copy-start.51
  896.6 1.5 copy-start.52
  898.1 1.3 copy-start.17
  898.1 1.5 copy-start.18
  899.6 2.6 copy-start.35
  899.6 2.6 copy-start.36
  899.6 2.6 copy-start.46
  1066.0 3.4 copy-start.13
  1069.3 2.5 copy-start.12
  1071.9 2.5 copy-start.11
  1071.9 3.9 copy-start.1
  (6 other events, 4.4 us)
Sparse Core Ops, SparseCore 0:
  13.8 31.2 all-gather.3
  47.2 28.5 all-gather.5
  243.8 53.0 all-gather.7
  427.7 66.6 reduce-scatter.6
  497.0 69.0 reduce-scatter.4
  789.1 36.0 reduce-scatter.8
  827.9 37.9 reduce-scatter.10
  872.8 193.1 all-reduce.3
